TPU v7x, 128 devices: a whole 4x4x4 slice. The times are simulated.
128 devices in a mesh: dp: 8 (over y, core), feat: 16 (over z, x).
Axes of the slice: x: 4, y: 4, z: 4, core: 2. Of those that a mesh axis runs over, the one named last changes fastest.
Arguments:
- features: bfloat16 [32768, 8192], P('dp', 'feat'), may hold values from -6 to 6
- fixed_coef: float32 [8192], P('feat'), may hold values from -0.0625 to 0.0625
- member_score: float32 [32768], P('dp'), may hold values from -6 to 6
- clicks: int32 [32768], P('dp'), may hold values 0 or 1
- member_features: bfloat16 [32768, 256], P(('dp', 'feat')), may hold values from -6 to 6
- member_coef: float32 [1024, 256], P(('dp', 'feat')), may hold values from -0.375 to 0.375
- block_slot: int32 [32768], P(('dp', 'feat')), may hold values from 0 to 65535, as said below
Outputs:
- fixed_grad: float32 [8192], P('feat')
- member_coef_new: float32 [1024, 256], P(('dp', 'feat'))
- total_score: float32 [32768], P(('dp', 'feat'))
Inputs may be any that keep to these rules, and one draw needn't show every extreme that they name: All block_slot values differ. block_slot // 512 is the device (index along dp+feat) that owns the impression's member, and block_slot // 64 is the member. Every owner receives exactly 256 impressions. One device sends at most 6 of its impressions to one owner, and every device sends exactly 6 to some owner.
All inputs are finite; a program needn't handle non-finite values. Where the computation divides by a largest or mean magnitude, that divisor is 1e-20 or more. No bound on the sum of `clicks` on one device may be relied on, other than what follows from the above.
Results may differ from a plain program's by a relative error of at most 0.0093.
Values may be sent and summed in bfloat16 or wider, within the bound.
A program may use at most 64 MiB of HBM per device.

v0:
```python
import math
import jax
import jax.numpy as jnp
from jax import lax
from jax.sharding import PartitionSpec as P

BLK = 64
NEWTON = 3
ridge_weight = 1.0
high = lax.Precision.HIGHEST
inverse_sweeps = 20


def apply_inverse(system, vector):
    identity = jnp.eye(system.shape[1], dtype=system.dtype)
    bound = jnp.max(jnp.sum(jnp.abs(system), axis=2), axis=1)
    start = (2.0 / (1.0 + bound))[:, None, None] * identity[None, :, :]

    def sweep(index, approx):
        product = jnp.einsum("mbc,mcd->mbd", system, approx, precision=high)
        return 2.0 * approx - jnp.einsum("mbc,mcd->mbd", approx, product, precision=high)

    approx = lax.fori_loop(0, inverse_sweeps, sweep, start)
    return jnp.einsum("mbc,mc->mb", approx, vector, precision=high)


def newton_blocks(padded_rows, offset, label_pad, live_pad, coeffs):
    gram_matrix = jnp.einsum("mbk,mck->mbc", padded_rows, padded_rows, precision=high)
    identity = jnp.eye(padded_rows.shape[1], dtype=padded_rows.dtype)
    for iteration in range(NEWTON):
        linear = offset + jnp.einsum("mbk,mk->mb", padded_rows, coeffs, precision=high)
        probability = jax.nn.sigmoid(linear)
        gradient = (
            jnp.einsum(
                "mbk,mb->mk", padded_rows, live_pad * (probability - label_pad), precision=high
            )
            + ridge_weight * coeffs
        )
        weight_root = jnp.sqrt(live_pad * probability * (1.0 - probability))
        system = (
            ridge_weight * identity
            + weight_root[:, :, None] * gram_matrix * weight_root[:, None, :]
        )
        projected = weight_root * jnp.einsum("mbk,mk->mb", padded_rows, gradient, precision=high)
        solved = apply_inverse(system, projected)
        back_term = jnp.einsum("mbk,mb->mk", padded_rows, weight_root * solved, precision=high)
        coeffs = coeffs - (gradient - back_term) / ridge_weight
    return coeffs


def per_device(
    features, fixed_coef, member_score, clicks, member_features, member_coef, block_slot
):
    n_dp = lax.axis_size("dp")
    n_feat = lax.axis_size("feat")
    devices = n_dp * n_feat
    rows_own = member_features.shape[0]
    width = member_features.shape[1]
    slot_count = 2 * rows_own
    blocks = slot_count // BLK
    capacity = 3 * ((rows_own + devices - 1) // devices)
    row_start = lax.axis_index("feat") * rows_own
    coef_half = fixed_coef.astype(jnp.bfloat16)
    partial_score = jnp.dot(features, coef_half, preferred_element_type=jnp.float32)
    own_clicks = lax.dynamic_slice_in_dim(clicks, row_start, rows_own).astype(jnp.float32)
    fixed_score = lax.psum(partial_score, "feat")
    residual = (jax.nn.sigmoid(fixed_score + member_score) - clicks.astype(jnp.float32)).astype(
        jnp.bfloat16
    )
    own_score = lax.dynamic_slice_in_dim(fixed_score, row_start, rows_own)
    grad_part = jnp.dot(residual, features, preferred_element_type=jnp.float32)
    fixed_grad = lax.psum(grad_part, "dp") / math.sqrt(rows_own * devices)
    owner_dev = block_slot // slot_count
    local_slot = block_slot - owner_dev * slot_count
    onehot = (owner_dev[:, None] == jnp.arange(devices, dtype=jnp.int32)[None, :]).astype(jnp.int32)
    row_rank = jnp.sum(jnp.cumsum(onehot, axis=0) * onehot, axis=1) - 1
    send_place = owner_dev * capacity + row_rank
    rows_out = (
        jnp.zeros((devices * capacity, width), jnp.bfloat16).at[send_place].set(member_features)
    )
    tag_value = (local_slot * 2).astype(jnp.float32) + own_clicks
    score_buffer = jnp.zeros((devices * capacity,), jnp.float32).at[send_place].set(own_score)
    tag_buffer = jnp.full((devices * capacity,), -1.0, jnp.float32).at[send_place].set(tag_value)
    meta_out = jnp.stack([score_buffer, tag_buffer])
    rows_in = lax.all_to_all(
        rows_out.reshape(devices, capacity, width),
        ("dp", "feat"),
        split_axis=0,
        concat_axis=0,
        tiled=True,
    )
    meta_in = lax.all_to_all(
        meta_out.reshape(2, devices, capacity),
        ("dp", "feat"),
        split_axis=1,
        concat_axis=1,
        tiled=True,
    )
    rows_in = rows_in.reshape(devices * capacity, width)
    meta_in = meta_in.reshape(2, devices * capacity)
    tags_in = meta_in[1]
    valid_slot = tags_in >= 0.0
    tag_int = jnp.where(valid_slot, tags_in, 0.0).astype(jnp.int32)
    label_in = (tag_int % 2).astype(jnp.float32)
    where_local = jnp.where(valid_slot, tag_int // 2, slot_count)
    padded_rows = (
        jnp.zeros((slot_count + 1, width), jnp.float32)
        .at[where_local]
        .set(rows_in.astype(jnp.float32))[:slot_count]
        .reshape(blocks, BLK, width)
    )
    offset = (
        jnp.zeros((slot_count + 1,), jnp.float32)
        .at[where_local]
        .set(meta_in[0])[:slot_count]
        .reshape(blocks, BLK)
    )
    label_pad = (
        jnp.zeros((slot_count + 1,), jnp.float32)
        .at[where_local]
        .set(label_in)[:slot_count]
        .reshape(blocks, BLK)
    )
    live_pad = (
        jnp.zeros((slot_count + 1,), jnp.float32)
        .at[where_local]
        .set(1.0)[:slot_count]
        .reshape(blocks, BLK)
    )
    coeffs = newton_blocks(padded_rows, offset, label_pad, live_pad, member_coef)
    member_value = jnp.einsum("mbk,mk->mb", padded_rows, coeffs, precision=high).reshape(slot_count)
    back_value = jnp.where(valid_slot, member_value[jnp.minimum(where_local, slot_count - 1)], 0.0)
    returned = lax.all_to_all(
        back_value.reshape(devices, capacity),
        ("dp", "feat"),
        split_axis=0,
        concat_axis=0,
        tiled=True,
    )
    returned = returned.reshape(devices * capacity)
    total_score = own_score + returned[send_place]
    return (fixed_grad, coeffs, total_score)


def solution(mesh):
    return jax.shard_map(
        per_device,
        mesh=mesh,
        in_specs=(
            P("dp", "feat"),
            P("feat"),
            P("dp"),
            P("dp"),
            P(("dp", "feat"), None),
            P(("dp", "feat"), None),
            P(("dp", "feat")),
        ),
        out_specs=(P("feat"), P(("dp", "feat"), None), P(("dp", "feat"))),
        check_vma=False,
    )
```

profile of v0, /device:TPU:1, one launch (start us, length us, event | category | flops | bytes accessed | tf_op | source)
XLA Modules:
  0.0 235.6 jit_solution(464150204069671483)
XLA Ops:
  0.7 0.8 convert_add_fusion
  2.1 0.7 convert_element_type.65
  2.8 3.4 %fusion.54 = f32[1,4096]{1,0:T(1,128)S(1)} fusion(bf16[4096,512]{1,0:T(8,128)(2,1)} %param.13, bf16[512,1]{0,1:T(2,128)(2,1)S(1)} %reshape.293), kind=kOutput, calls=%fused_computation.124 | convolution fusion | flops 4194304 | bytes 4211712 | tf_op jit(solution)/shard_map/dot_general | solution.py:64
  6.1 62.3 %psum.14 = f32[4096]{0:T(1024)S(1)} all-reduce(f32[4096]{0:T(1024)S(1)} %bitcast.212), channel_id=1, replica_groups=mesh['dp'=8,'feat'=16] {'feat'}, use_global_device_ids=true, to_apply=%region_0.0 | all-reduce | flops 4096 | bytes 32768 | tf_op jit(solution)/shard_map/psum | solution.py:66
  68.5 1.4 scatter_custom_fusion
  70.0 1.4 scatter_custom_fusion.1
  71.6 0.8 copy.54
  72.3 18.9 %all-to-all-start = ((f32[2,128,6]{2,0,1:T(2,128)}), f32[2,128,6]{2,0,1:T(2,128)S(1)}, u32[]{:S(2)}, u32[]{:S(2)}) async-start(f32[2,128,6]{2,0,1:T(2,128)} %copy.54), calls=%async_computation | async-start | bytes 262144 | tf_op jit(solution)/shard_map/all_to_all | solution.py:92
  91.3 2.8 %fusion.55 = f32[1,512]{1,0:T(1,128)S(1)} fusion(bf16[4096,1]{0,1:T(2,128)(2,1)S(1)} %reshape.295, bf16[4096,512]{1,0:T(8,128)(2,1)} %param.13), kind=kOutput, calls=%fused_computation.125 | convolution fusion | flops 4194304 | bytes 4204544 | tf_op jit(solution)/shard_map/dot_general | solution.py:71
  94.2 12.8 %psum.15 = f32[512]{0:T(512)S(1)} all-reduce(f32[512]{0:T(512)S(1)} %bitcast.239), channel_id=1, replica_groups=mesh['dp'=8,'feat'=16] {'dp'}, use_global_device_ids=true, to_apply=%region_1.0 | all-reduce | flops 512 | bytes 4096 | tf_op jit(solution)/shard_map/psum | solution.py:72
  107.0 0.6 broadcast_multiply_fusion.3
  107.6 2.0 scatter_custom_fusion.2
  109.6 0.9 reshape.209
  110.5 9.4 %all-to-all-start.1 = ((bf16[128,6,256]{2,1,0:T(8,128)(2,1)}), bf16[128,6,256]{2,1,0:T(8,128)(2,1)S(1)}, u32[]{:S(2)}, u32[]{:S(2)}) async-start(bf16[128,6,256]{2,1,0:T(8,128)(2,1)} %reshape.209), calls=%async_computation.1 | async-start | bytes 1048576 | tf_op jit(solution)/shard_map/all_to_all | solution.py:85
  120.5 3.4 %scatter_custom_fusion.6 = f32[513]{0:T(1024)S(1)} fusion(s32[768]{0:T(1024)S(1)} %get-tuple-element.94, f32[768]{0:T(1024)S(1)} %fusion.33, f32[]{:T(128)} %constant.51.clone.1), kind=kCustom, calls=%fused_computation.98 | custom fusion | bytes 2056 | tf_op jit(solution)/shard_map/scatter | solution.py:121
  124.1 3.4 %scatter_custom_fusion.5 = f32[513]{0:T(1024)S(1)} fusion(s32[768]{0:T(1024)S(1)} %get-tuple-element.94, f32[768]{0:T(1024)S(1)} %reshape.277, f32[]{:T(128)} %constant.51.clone.1), kind=kCustom, calls=%fused_computation.100 | custom fusion | bytes 2056 | tf_op jit(solution)/shard_map/scatter | solution.py:115
  127.6 3.6 %scatter_custom_fusion.4 = f32[513]{0:T(1024)S(1)} fusion(s32[768]{0:T(1024)S(1)} %get-tuple-element.94, f32[768]{0:T(1024)S(1)} %broadcast.285, f32[]{:T(128)} %constant.51.clone.1), kind=kCustom, calls=%fused_computation.102 | custom fusion | bytes 2056 | tf_op jit(solution)/shard_map/scatter | solution.py:127
  131.2 2.8 %all-to-all-done.1 = bf16[128,6,256]{2,1,0:T(8,128)(2,1)S(1)} async-done(((bf16[128,6,256]{2,1,0:T(8,128)(2,1)}), bf16[128,6,256]{2,1,0:T(8,128)(2,1)S(1)}, u32[]{:S(2)}, u32[]{:S(2)}) %all-to-all-start.1) | async-done | bytes 393248 | tf_op jit(solution)/shard_map/all_to_all | solution.py:85
  134.1 5.6 %scatter_custom_fusion.3 = f32[513,256]{1,0:T(8,128)S(1)} fusion(s32[768]{0:T(1024)S(1)} %get-tuple-element.94, f32[768,256]{1,0:T(8,128)S(1)} %reshape.261, f32[]{:T(128)} %constant.51.clone.1), kind=kCustom, calls=%fused_computation.15 | custom fusion | bytes 525316 | tf_op jit(solution)/shard_map/scatter | solution.py:109
  139.8 0.6 fusion.27
  141.4 0.6 abs_reduce_fusion.2
  142.4 20.0 %while.30 = (s32[]{:T(128)}, f32[8,64,64]{1,2,0:T(8,128)S(1)}, f32[8,64,64]{2,1,0:T(8,128)S(1)}, s32[]{:T(128)}) while((s32[]{:T(128)}, f32[8,64,64]{1,2,0:T(8,128)S(1)}, f32[8,64,64]{2,1,0:T(8,128)S(1)}, s32[]{:T(128)}) %tuple.70), condition=%wide.region_15.16_spmd, body=%wide.region_14.15_spmd.sunk | while | flops 50397184 | bytes 1048629 | solution.py:23
  163.1 0.6 fusion.23
  165.2 20.0 %while.31 = (s32[]{:T(128)}, f32[8,64,64]{1,2,0:T(8,128)S(1)}, f32[8,64,64]{2,1,0:T(8,128)S(1)}, s32[]{:T(128)}) while((s32[]{:T(128)}, f32[8,64,64]{1,2,0:T(8,128)S(1)}, f32[8,64,64]{2,1,0:T(8,128)S(1)}, s32[]{:T(128)}) %tuple.73), condition=%wide.region_19.20_spmd, body=%wide.region_18.19_spmd.sunk | while | flops 50397184 | bytes 1048629 | solution.py:23
  188.1 20.0 %while.32 = (s32[]{:T(128)}, f32[8,64,64]{1,2,0:T(8,128)S(1)}, f32[8,64,64]{2,1,0:T(8,128)S(1)}, s32[]{:T(128)}) while((s32[]{:T(128)}, f32[8,64,64]{1,2,0:T(8,128)S(1)}, f32[8,64,64]{2,1,0:T(8,128)S(1)}, s32[]{:T(128)}) %tuple.76), condition=%wide.region_23.24_spmd, body=%wide.region_22.23_spmd.sunk | while | flops 50397184 | bytes 1048629 | solution.py:23
  209.5 5.0 %gather_fusion = f32[768]{0:T(1024)S(1)} fusion(f32[512]{0:T(512)S(1)} %reshape.214, s32[1024]{0:T(1024)S(1)} %pad_clamp_fusion.1), kind=kCustom, calls=%fused_computation | custom fusion | bytes 9216 | tf_op jit(solution)/shard_map/gather | solution.py:132
  214.7 0.6 bitcast_select_fusion.1
  215.3 7.0 %all-to-all-start.2 = ((f32[128,1,6]{2,1,0:T(1,128)}), f32[128,1,6]{2,1,0:T(1,128)S(1)}, u32[]{:S(2)}, u32[]{:S(2)}) async-start(f32[128,1,6]{2,1,0:T(1,128)} %bitcast.62), calls=%async_computation.2 | async-start | bytes 131072 | tf_op jit(solution)/shard_map/all_to_all | solution.py:133
  222.3 9.8 %all-to-all-done.2 = f32[128,1,6]{2,1,0:T(1,128)S(1)} async-done(((f32[128,1,6]{2,1,0:T(1,128)}), f32[128,1,6]{2,1,0:T(1,128)S(1)}, u32[]{:S(2)}, u32[]{:S(2)}) %all-to-all-start.2) | async-done | bytes 3104 | tf_op jit(solution)/shard_map/all_to_all | solution.py:133
  232.6 0.8 reduce.11
  233.6 1.4 gather_fusion.1
  234.9 0.6 dynamic-slice_add_fusion
  (271 shorter events, 68.3 us)
Async XLA Ops:
  0.6 90.6 %copy-start.2 = (s32[4096]{0:T(1024)S(1)}, s32[4096]{0:T(1024)}, u32[]{:S(2)}) copy-start(s32[4096]{0:T(1024)} %param.16) | copy-start | bytes 49156
  0.6 90.6 %copy-start.3 = (f32[4096]{0:T(1024)S(1)}, f32[4096]{0:T(1024)}, u32[]{:S(2)}) copy-start(f32[4096]{0:T(1024)} %param.15) | copy-start | bytes 49156
  72.3 38.2 %all-to-all-start = ((f32[2,128,6]{2,0,1:T(2,128)}), f32[2,128,6]{2,0,1:T(2,128)S(1)}, u32[]{:S(2)}, u32[]{:S(2)}) async-start(f32[2,128,6]{2,0,1:T(2,128)} %copy.54), calls=%async_computation | async-start | bytes 262144 | tf_op jit(solution)/shard_map/all_to_all | solution.py:92
  91.3 48.4 %copy-start = (f32[8,256]{1,0:T(8,128)S(1)}, f32[8,256]{1,0:T(8,128)}, u32[]{:S(2)}) copy-start(f32[8,256]{1,0:T(8,128)} %param.18) | copy-start | bytes 24580
  110.5 23.5 %all-to-all-start.1 = ((bf16[128,6,256]{2,1,0:T(8,128)(2,1)}), bf16[128,6,256]{2,1,0:T(8,128)(2,1)S(1)}, u32[]{:S(2)}, u32[]{:S(2)}) async-start(bf16[128,6,256]{2,1,0:T(8,128)(2,1)} %reshape.209), calls=%async_computation.1 | async-start | bytes 1048576 | tf_op jit(solution)/shard_map/all_to_all | solution.py:85
  208.9 26.7 %copy-start.1 = (f32[8,256]{1,0:T(8,128)}, f32[8,256]{1,0:T(8,128)S(1)}, u32[]{:S(2)}) copy-start(f32[8,256]{1,0:T(8,128)S(1)} %fusion.12) | copy-start | bytes 24580
  215.3 16.8 %all-to-all-start.2 = ((f32[128,1,6]{2,1,0:T(1,128)}), f32[128,1,6]{2,1,0:T(1,128)S(1)}, u32[]{:S(2)}, u32[]{:S(2)}) async-start(f32[128,1,6]{2,1,0:T(1,128)} %bitcast.62), calls=%async_computation.2 | async-start | bytes 131072 | tf_op jit(solution)/shard_map/all_to_all | solution.py:133
where the time goes:
time: 236 us
  blocking collectives  75.1 us (32%)
  matrix products  70.7 us (30%)
  starting transfers between devices  35.3 us (15%)
  local copies, waits for them, and re-layouts  32.6 us (14%)
  waiting for transfers between devices  12.6 us (5%)
  other arithmetic  5.86 us (2%)
    psum x1, blocking collectives, per_device(): fixed_score = lax.psum(partial_score, 'feat')  62.3 us
    dot_general x60, matrix products, sweep(): product = jnp.einsum('mbc,mcd->mbd', system, approx, precision=high)  32.8 us
    dot_general x60, matrix products, sweep(): jnp.einsum('mbc,mcd->mbd', approx, product, precision=high)  23.8 us
    all_to_all x1, starting transfers between devices, per_device(): lax.all_to_all(meta_out.reshape(2, devices, capacity), ('dp', 'feat'), sp...  18.9 us
    psum x1, blocking collectives, per_device(): fixed_grad = lax.psum(grad_part, 'dp') / math.sqrt(rows_own * devices)  12.8 us
    all_to_all x1, waiting for transfers between devices, per_device(): lax.all_to_all(back_value.reshape(devices, capacity), ('dp', 'feat'), spl...  9.8 us
    all_to_all x1, starting transfers between devices, per_device(): lax.all_to_all(rows_out.reshape(devices, capacity, width), ('dp', 'feat')...  9.4 us
    all_to_all x1, starting transfers between devices, per_device(): lax.all_to_all(back_value.reshape(devices, capacity), ('dp', 'feat'), spl...  6.99 us
  transfers between devices with their start and end apart: 3, of which 2 were waited for; matrix products, arithmetic and copies ran while one was open for 7% of the time, Pallas kernels for 0%

commit v1 on v0

--- a/solution.py
+++ b/solution.py
@@ -1,3 +1,4 @@
+import functools
 import math
 import jax
 import jax.numpy as jnp
@@ -9,6 +10,15 @@
 ridge_weight = 1.0
 high = lax.Precision.HIGHEST
 inverse_sweeps = 20
+
+
+def threads_keep_up(slab_in, axis_k, on_dim):
+    local_next = jnp.stack(jnp.split(slab_in, lax.axis_size(("dp", "feat")), axis_k))
+    z_new = lax.all_to_all(local_next, ("dp", "feat"), 0, 0)
+    return jnp.concatenate(z_new, on_dim)
+
+
+arrange_stacks_all_in = functools.partial(threads_keep_up, axis_k=1, on_dim=1)
 
 
 def apply_inverse(system, vector):
@@ -89,13 +99,7 @@
         concat_axis=0,
         tiled=True,
     )
-    meta_in = lax.all_to_all(
-        meta_out.reshape(2, devices, capacity),
-        ("dp", "feat"),
-        split_axis=1,
-        concat_axis=1,
-        tiled=True,
-    )
+    meta_in = arrange_stacks_all_in(meta_out.reshape(2, devices, capacity))
     rows_in = rows_in.reshape(devices * capacity, width)
     meta_in = meta_in.reshape(2, devices * capacity)
     tags_in = meta_in[1]

time: 236 us -> 323 us (1.37)
  local copies, waits for them, and re-layouts: 32.6 us -> 118 us
    unnamed x9 -> x136, local copies, waits for them, and re-layouts: 0.03 us -> 72.5 us
    split x0 -> x128, local copies, waits for them, and re-layouts: none -> 12.5 us  [threads_keep_up(): jnp.split(slab_in, lax.axis_size(('dp', 'feat')), axis_k)]
  transfers between devices with their start and end apart: 3 -> 3, of which waited for: 2 -> 2; matrix products, arithmetic and copies ran while one was open for 7% -> 5% of each run, Pallas kernels for 0% -> 0%
where the time goes in v1:
time: 323 us
  local copies, waits for them, and re-layouts  118 us (37%)
  blocking collectives  75.1 us (23%)
  matrix products  70.3 us (22%)
  starting transfers between devices  35.2 us (11%)
  waiting for transfers between devices  12.7 us (4%)
  other arithmetic  7.83 us (2%)
    unnamed x136, local copies, waits for them, and re-layouts  72.5 us
    psum x1, blocking collectives, per_device(): fixed_score = lax.psum(partial_score, 'feat')  62.3 us
    dot_general x60, matrix products, sweep(): product = jnp.einsum('mbc,mcd->mbd', system, approx, precision=high)  32.7 us
    dot_general x60, matrix products, sweep(): jnp.einsum('mbc,mcd->mbd', approx, product, precision=high)  23.4 us
    all_to_all x1, starting transfers between devices, threads_keep_up(): z_new = lax.all_to_all(local_next, ('dp', 'feat'), 0, 0)  18.9 us
    psum x1, blocking collectives, per_device(): fixed_grad = lax.psum(grad_part, 'dp') / math.sqrt(rows_own * devices)  12.8 us
    split x128, local copies, waits for them, and re-layouts, threads_keep_up(): jnp.split(slab_in, lax.axis_size(('dp', 'feat')), axis_k)  12.5 us
    all_to_all x1, waiting for transfers between devices, per_device(): lax.all_to_all(back_value.reshape(devices, capacity), ('dp', 'feat'), spl...  9.8 us
  transfers between devices with their start and end apart: 3, of which 2 were waited for; matrix products, arithmetic and copies ran while one was open for 5% of the time, Pallas kernels for 0%

profile of v1, /device:TPU:1, one launch (start us, length us, event | category | flops | bytes accessed | tf_op | source)
XLA Modules:
  0.0 323.0 jit_solution(7416826848060790800)
XLA Ops:
  0.6 0.8 convert_add_fusion
  2.0 0.7 convert_element_type.65
  2.7 3.4 %fusion.182 = f32[1,4096]{1,0:T(1,128)S(1)} fusion(bf16[4096,512]{1,0:T(8,128)(2,1)} %param.13, bf16[512,1]{0,1:T(2,128)(2,1)S(1)} %reshape.296), kind=kOutput, calls=%fused_computation.633 | convolution fusion | flops 4194304 | bytes 4211712 | tf_op jit(solution)/shard_map/dot_general | solution.py:74
  6.1 62.3 %psum.14 = f32[4096]{0:T(1024)S(1)} all-reduce(f32[4096]{0:T(1024)S(1)} %bitcast.477), channel_id=1, replica_groups=mesh['dp'=8,'feat'=16] {'feat'}, use_global_device_ids=true, to_apply=%region_0.0 | all-reduce | flops 4096 | bytes 32768 | tf_op jit(solution)/shard_map/psum | solution.py:76
  68.4 1.4 scatter_custom_fusion
  70.0 1.4 scatter_custom_fusion.1
  74.5 0.6 constant_dynamic-update-slice_fusion.127
  104.7 0.6 constant_dynamic-update-slice_fusion.96
  121.8 0.6 constant_dynamic-update-slice_fusion.66
  124.2 0.6 constant_dynamic-update-slice_fusion.62
  160.1 18.9 %all-to-all-start = ((f32[128,2,1,6]{3,2,1,0:T(1,128)}), f32[128,2,1,6]{3,2,1,0:T(1,128)S(1)}, u32[]{:S(2)}, u32[]{:S(2)}) async-start(f32[128,2,1,6]{3,2,1,0:T(1,128)} %bitcast.137), calls=%async_computation | async-start | bytes 262144 | tf_op jit(solution)/shard_map/all_to_all | solution.py:17
  179.1 2.8 fusion.183
  181.9 12.8 %psum.15 = f32[512]{0:T(512)S(1)} all-reduce(f32[512]{0:T(512)S(1)} %bitcast.506), channel_id=1, replica_groups=mesh['dp'=8,'feat'=16] {'dp'}, use_global_device_ids=true, to_apply=%region_1.0 | all-reduce | flops 512 | bytes 4096 | tf_op jit(solution)/shard_map/psum | solution.py:82
  195.4 2.0 scatter_custom_fusion.2
  197.3 0.9 reshape.212
  198.3 9.4 %all-to-all-start.1 = ((bf16[128,6,256]{2,1,0:T(8,128)(2,1)}), bf16[128,6,256]{2,1,0:T(8,128)(2,1)S(1)}, u32[]{:S(2)}, u32[]{:S(2)}) async-start(bf16[128,6,256]{2,1,0:T(8,128)(2,1)} %reshape.212), calls=%async_computation.1 | async-start | bytes 1048576 | tf_op jit(solution)/shard_map/all_to_all | solution.py:95
  208.5 3.4 %scatter_custom_fusion.5 = f32[513]{0:T(1024)S(1)} fusion(s32[768]{0:T(1024)S(1)} %get-tuple-element.103, f32[768]{0:T(1024)S(1)} %reshape.280, f32[]{:T(128)} %constant.51.clone.1), kind=kCustom, calls=%fused_computation.608 | custom fusion | bytes 2056 | tf_op jit(solution)/shard_map/scatter | solution.py:119
  212.0 3.4 %scatter_custom_fusion.6 = f32[513]{0:T(1024)S(1)} fusion(s32[768]{0:T(1024)S(1)} %get-tuple-element.103, f32[768]{0:T(1024)S(1)} %fusion.160, f32[]{:T(128)} %constant.51.clone.1), kind=kCustom, calls=%fused_computation.606 | custom fusion | bytes 2056 | tf_op jit(solution)/shard_map/scatter | solution.py:125
  215.4 3.4 %scatter_custom_fusion.4 = f32[513]{0:T(1024)S(1)} fusion(s32[768]{0:T(1024)S(1)} %get-tuple-element.103, f32[768]{0:T(1024)S(1)} %broadcast.285, f32[]{:T(128)} %constant.51.clone.1), kind=kCustom, calls=%fused_computation.610 | custom fusion | bytes 2056 | tf_op jit(solution)/shard_map/scatter | solution.py:131
  218.9 2.9 all-to-all-done.1
  221.9 5.6 %scatter_custom_fusion.3 = f32[513,256]{1,0:T(8,128)S(1)} fusion(s32[768]{0:T(1024)S(1)} %get-tuple-element.103, f32[768,256]{1,0:T(8,128)S(1)} %reshape.264, f32[]{:T(128)} %constant.51.clone.1), kind=kCustom, calls=%fused_computation.15 | custom fusion | bytes 525316 | tf_op jit(solution)/shard_map/scatter | solution.py:113
  229.1 0.6 abs_reduce_fusion.2
  230.1 19.9 %while.30 = (s32[]{:T(128)}, f32[8,64,64]{1,2,0:T(8,128)S(1)}, f32[8,64,64]{2,1,0:T(8,128)S(1)}, s32[]{:T(128)}) while((s32[]{:T(128)}, f32[8,64,64]{1,2,0:T(8,128)S(1)}, f32[8,64,64]{2,1,0:T(8,128)S(1)}, s32[]{:T(128)}) %tuple.186), condition=%wide.region_15.16_spmd, body=%wide.region_14.15_spmd.sunk | while | flops 50397184 | bytes 1048629 | solution.py:33
  252.9 19.9 %while.31 = (s32[]{:T(128)}, f32[8,64,64]{1,2,0:T(8,128)S(1)}, f32[8,64,64]{2,1,0:T(8,128)S(1)}, s32[]{:T(128)}) while((s32[]{:T(128)}, f32[8,64,64]{1,2,0:T(8,128)S(1)}, f32[8,64,64]{2,1,0:T(8,128)S(1)}, s32[]{:T(128)}) %tuple.189), condition=%wide.region_19.20_spmd, body=%wide.region_18.19_spmd.sunk | while | flops 50397184 | bytes 1048629 | solution.py:33
  275.6 19.9 %while.32 = (s32[]{:T(128)}, f32[8,64,64]{1,2,0:T(8,128)S(1)}, f32[8,64,64]{2,1,0:T(8,128)S(1)}, s32[]{:T(128)}) while((s32[]{:T(128)}, f32[8,64,64]{1,2,0:T(8,128)S(1)}, f32[8,64,64]{2,1,0:T(8,128)S(1)}, s32[]{:T(128)}) %tuple.192), condition=%wide.region_23.24_spmd, body=%wide.region_22.23_spmd.sunk | while | flops 50397184 | bytes 1048629 | solution.py:33
  296.9 5.0 %gather_fusion = f32[768]{0:T(1024)S(1)} fusion(f32[512]{0:T(512)S(1)} %reshape.217, s32[1024]{0:T(1024)S(1)} %pad_clamp_fusion.1), kind=kCustom, calls=%fused_computation | custom fusion | bytes 9216 | tf_op jit(solution)/shard_map/gather | solution.py:136
  302.1 0.8 copy.734
  302.8 6.9 %all-to-all-start.2 = ((f32[128,1,6]{2,1,0:T(1,128)}), f32[128,1,6]{2,1,0:T(1,128)S(1)}, u32[]{:S(2)}, u32[]{:S(2)}) async-start(f32[128,1,6]{2,1,0:T(1,128)} %copy.734), calls=%async_computation.2 | async-start | bytes 131072 | tf_op jit(solution)/shard_map/all_to_all | solution.py:137
  309.8 9.8 %all-to-all-done.2 = f32[128,1,6]{2,1,0:T(1,128)S(1)} async-done(((f32[128,1,6]{2,1,0:T(1,128)}), f32[128,1,6]{2,1,0:T(1,128)S(1)}, u32[]{:S(2)}, u32[]{:S(2)}) %all-to-all-start.2) | async-done | bytes 3104 | tf_op jit(solution)/shard_map/all_to_all | solution.py:137
  320.1 0.8 reduce.7
  321.0 1.4 gather_fusion.1
  322.4 0.6 dynamic-slice_add_fusion
  (547 shorter events, 155.7 us)
Async XLA Ops:
  2.7 176.3 %copy-start.2 = (s32[4096]{0:T(1024)S(1)}, s32[4096]{0:T(1024)}, u32[]{:S(2)}) copy-start(s32[4096]{0:T(1024)} %param.16) | copy-start | bytes 49156
  2.7 176.3 %copy-start.3 = (f32[4096]{0:T(1024)S(1)}, f32[4096]{0:T(1024)}, u32[]{:S(2)}) copy-start(f32[4096]{0:T(1024)} %param.15) | copy-start | bytes 49156
  160.1 38.2 %all-to-all-start = ((f32[128,2,1,6]{3,2,1,0:T(1,128)}), f32[128,2,1,6]{3,2,1,0:T(1,128)S(1)}, u32[]{:S(2)}, u32[]{:S(2)}) async-start(f32[128,2,1,6]{3,2,1,0:T(1,128)} %bitcast.137), calls=%async_computation | async-start | bytes 262144 | tf_op jit(solution)/shard_map/all_to_all | solution.py:17
  179.1 48.4 %copy-start = (f32[8,256]{1,0:T(8,128)S(1)}, f32[8,256]{1,0:T(8,128)}, u32[]{:S(2)}) copy-start(f32[8,256]{1,0:T(8,128)} %param.18) | copy-start | bytes 24580
  198.3 23.5 %all-to-all-start.1 = ((bf16[128,6,256]{2,1,0:T(8,128)(2,1)}), bf16[128,6,256]{2,1,0:T(8,128)(2,1)S(1)}, u32[]{:S(2)}, u32[]{:S(2)}) async-start(bf16[128,6,256]{2,1,0:T(8,128)(2,1)} %reshape.212), calls=%async_computation.1 | async-start | bytes 1048576 | tf_op jit(solution)/shard_map/all_to_all | solution.py:95
  296.2 26.8 %copy-start.1 = (f32[8,256]{1,0:T(8,128)}, f32[8,256]{1,0:T(8,128)S(1)}, u32[]{:S(2)}) copy-start(f32[8,256]{1,0:T(8,128)S(1)} %fusion.12) | copy-start | bytes 24580
  302.8 16.7 %all-to-all-start.2 = ((f32[128,1,6]{2,1,0:T(1,128)}), f32[128,1,6]{2,1,0:T(1,128)S(1)}, u32[]{:S(2)}, u32[]{:S(2)}) async-start(f32[128,1,6]{2,1,0:T(1,128)} %copy.734), calls=%async_computation.2 | async-start | bytes 131072 | tf_op jit(solution)/shard_map/all_to_all | solution.py:137
